TPU v7x, 32 devices: a whole 2x2x4 slice. The times are simulated.
32 devices in a mesh: lat: 4 (over y, x), lon: 8 (over z, core).
Axes of the slice: x: 2, y: 2, z: 4, core: 2. Of those that a mesh axis runs over, the one named last changes fastest.
Arguments:
- right_side: float32 [512, 2048], P('lat', 'lon'), may hold values from -12 to 12
- diagonal: float32 [512, 2048], P('lat', 'lon'), may hold values from 0.2 to 2
- east_coef: float32 [512, 2048], P('lat', 'lon'), may hold values from 0.5 to 2
- north_coef: float32 [512, 2048], P('lat', 'lon'), may hold values from 0.5 to 2
- land_sea: int32 [512, 2048], P('lat', 'lon'), may hold values 0 or 1
- fold_partner: int32 [2048], P('lon'), may hold values from 0 to 2047, as said below
Outputs:
- solution_field: float32 [512, 2048], P('lat', 'lon')
- residual: float32 [512, 2048], P('lat', 'lon')
Inputs may be any that keep to these rules, and one draw needn't show every extreme that they name: fold_partner[fold_partner[i]] = i and fold_partner[i] != i for every column i, and fold_partner[i] // 256 = 7 - i // 256.
All inputs are finite; a program needn't handle non-finite values. No bound on the sum of `land_sea` on one device may be relied on, other than what follows from the above.
Results may differ from a plain program's by a relative error of at most 0.00019.
Values sent between devices are 32-bit elements; how exact they have to be, the bound alone decides.
A program may use at most 64 MiB of HBM per device.

v0:
```python
import jax
import jax.numpy as jnp
from jax import lax
from jax.sharding import PartitionSpec as P

ITERS = 4


def with_halo(cells, sides, width, closed):
    for axis, dim in sides:
        count = lax.axis_size(axis)
        ends = count if closed else count - 1
        head = lax.slice_in_dim(cells, 0, width, axis=dim)
        tail = lax.slice_in_dim(cells, cells.shape[dim] - width, cells.shape[dim], axis=dim)
        cells = jnp.concatenate(
            [
                lax.ppermute(tail, axis, [(i, (i + 1) % count) for i in range(ends)]),
                cells,
                lax.ppermute(head, axis, [((i + 1) % count, i) for i in range(ends)]),
            ],
            axis=dim,
        )
    return cells


def zonal_rim(values):
    return with_halo(values, (("lon", 1),), 1, True)


def meridional_rim(values):
    return with_halo(values, (("lat", 0),), 1, False)


def paired(residual, image):
    return lax.psum((jnp.sum(residual * residual), jnp.sum(residual * image)), ("lat", "lon"))


def local(right_side, diagonal, east_coef, north_coef, land_sea, fold_partner):
    row_count, col_count = right_side.shape
    ocean = land_sea.astype(jnp.float32)
    on_top = lax.axis_index("lat") == lax.axis_size("lat") - 1
    row_ids = lax.broadcasted_iota(jnp.int32, (row_count, col_count), 0)
    north_inner = jnp.where(on_top & (row_ids == row_count - 1), 0.0, north_coef)
    west_coef = zonal_rim(east_coef)[:, :col_count]
    south_coef = meridional_rim(north_inner)[:row_count]

    def neighbours(masked):
        across_lon = zonal_rim(masked)
        across_lat = meridional_rim(masked)
        return (
            across_lon[:, 2:],
            across_lon[:, :col_count],
            across_lat[2:],
            across_lat[:row_count],
        )

    def mirror_row(top_values):
        whole_row = lax.all_gather(top_values, "lon", axis=0, tiled=True)
        return jnp.take(whole_row, fold_partner, axis=0)

    top_coef = north_coef[row_count - 1]
    fold_coef = jnp.where(on_top, 0.5 * (top_coef + mirror_row(top_coef)), 0.0)

    def operate(surface):
        masked = ocean * surface
        east_vals, west_vals, north_vals, south_vals = neighbours(masked)
        spread = east_coef * (masked - east_vals) + west_coef * (masked - west_vals)
        spread = spread + north_inner * (masked - north_vals) + south_coef * (masked - south_vals)
        last_row = masked[row_count - 1]
        spread = spread.at[row_count - 1].add(fold_coef * (last_row - mirror_row(last_row)))
        return diagonal * surface + ocean * spread

    solution_field = jnp.zeros_like(right_side)
    residual = right_side
    image = operate(residual)
    norm_now, product = paired(residual, image)
    alpha = norm_now / product
    direction, along = (residual, image)
    for iteration in range(ITERS):
        solution_field = solution_field + alpha * direction
        residual = residual - alpha * along
        if iteration + 1 < ITERS:
            image = operate(residual)
            norm_next, product = paired(residual, image)
            ratio = norm_next / norm_now
            alpha = norm_next / (product - ratio * norm_next / alpha)
            direction = residual + ratio * direction
            along = image + ratio * along
            norm_now = norm_next
    return (solution_field, residual)


def solution(mesh):
    placed = (
        P("lat", "lon"),
        P("lat", "lon"),
        P("lat", "lon"),
        P("lat", "lon"),
        P("lat", "lon"),
        P("lon"),
    )
    return jax.shard_map(
        local,
        mesh=mesh,
        in_specs=placed,
        out_specs=(P("lat", "lon"), P("lat", "lon")),
        check_vma=False,
    )
```

profile of v0, /device:TPU:12, one launch (start us, length us, event | category | flops | bytes accessed | tf_op | source)
XLA Modules:
  0.0 291.9 jit_solution(6611212178361798222)
XLA Ops:
  0.6 1.0 slice.203
  1.6 0.0 collective-permute-start.1
  1.7 0.0 copy-start
  1.7 0.0 copy-start.1
  1.7 0.1 broadcast_select_fusion
  1.8 3.4 %collective-permute-start.4 = (f32[1,256]{1,0:T(1,128)S(1)}, f32[1,256]{1,0:T(1,128)S(1)}, u32[]{:S(2)}, u32[]{:S(2)}) collective-permute-start(f32[1,256]{1,0:T(1,128)S(1)} %slice.255), channel_id=1, source_target_pairs={{0,8},{8,16},{16,24},{1,9},{9,17},{17,25},{2,10},{10,18},{18,26},{... | collective-permute-start | bytes 3080 | tf_op jit(solution)/shard_map/ppermute | solution.py:17
  5.3 3.3 %collective-permute-start.3 = (f32[1,256]{1,0:T(1,128)S(1)}, f32[1,256]{1,0:T(1,128)S(1)}, u32[]{:S(2)}, u32[]{:S(2)}) collective-permute-start(f32[1,256]{1,0:T(1,128)S(1)} %get-tuple-element.87), channel_id=1, source_target_pairs={{8,0},{16,8},{24,16},{9,1},{17,9},{25,17},{10,2},{18,10},{26,18},{... | collective-permute-start | bytes 3080 | tf_op jit(solution)/shard_map/ppermute | solution.py:19
  8.6 2.5 collective-permute-start.5
  11.1 0.1 fusion.57
  11.2 0.9 collective-permute-start
  12.1 10.8 %all-gather.1 = f32[1,2048]{1,0:T(1,128)S(1)} all-gather(f32[1,256]{1,0:T(1,128)S(1)} %get-tuple-element.88), channel_id=3, replica_groups=mesh['lat'=4,'lon'=8] {'lon'}, dimensions={1}, use_global_device_ids=true | all-gather | bytes 9216 | tf_op jit(solution)/shard_map/all_gather | solution.py:58
  22.9 10.2 %all-gather = f32[1,2048]{1,0:T(1,128)S(1)} all-gather(f32[1,256]{1,0:T(1,128)S(1)} %slice.214), channel_id=2, replica_groups=mesh['lat'=4,'lon'=8] {'lon'}, dimensions={1}, use_global_device_ids=true | all-gather | bytes 9216 | tf_op jit(solution)/shard_map/all_gather | solution.py:58
  33.1 1.7 gather_fusion
  34.8 0.0 copy-start.3
  34.8 1.7 gather_fusion.1
  36.6 0.0 collective-permute-done.1
  36.6 0.4 collective-permute-start.2
  37.0 0.0 collective-permute-done
  37.0 3.3 %collective-permute-done.2 = f32[128,1]{1,0:T(8,128)S(1)} collective-permute-done((f32[128,1]{1,0:T(8,128)S(1)}, f32[128,1]{1,0:T(8,128)S(1)}, u32[]{:S(2)}, u32[]{:S(2)}) %collective-permute-start.2) | collective-permute-done | bytes 544 | tf_op jit(solution)/shard_map/ppermute | solution.py:17
  40.3 0.2 fusion.35
  40.6 0.7 multiply_reduce_fusion.6
  41.3 41.4 %all-reduce.3 = (f32[]{:T(128)}, f32[]{:T(128)}) all-reduce(f32[]{:T(128)} %get-tuple-element.58, f32[]{:T(128)} %get-tuple-element.57), channel_id=1, replica_groups=mesh['lat'=4,'lon'=8] {'lat','lon'}, use_global_device_ids=true, to_apply=%region_1.2 | all-reduce | flops 2 | bytes 16 | tf_op jit(solution)/shard_map/psum | solution.py:35
  84.1 8.3 %all-gather.2 = f32[1,2048]{1,0:T(1,128)S(1)} all-gather(f32[1,256]{1,0:T(1,128)S(1)} %get-tuple-element.84), channel_id=4, replica_groups=mesh['lat'=4,'lon'=8] {'lon'}, dimensions={1}, use_global_device_ids=true | all-gather | bytes 9216 | tf_op jit(solution)/shard_map/all_gather | solution.py:58
  92.4 3.8 %collective-permute-start.9 = (f32[1,256]{1,0:T(1,128)S(1)}, f32[1,256]{1,0:T(1,128)S(1)}, u32[]{:S(2)}, u32[]{:S(2)}) collective-permute-start(f32[1,256]{1,0:T(1,128)S(1)} %get-tuple-element.84), channel_id=1, source_target_pairs={{0,8},{8,16},{16,24},{1,9},{9,17},{17,25},{2,10},{10,18},{18,26},{... | collective-permute-start | bytes 3080 | tf_op jit(solution)/shard_map/ppermute | solution.py:17
  96.2 0.1 fusion.55
  96.3 1.7 gather_fusion.2
  98.1 2.9 collective-permute-start.8
  101.0 1.5 collective-permute-start.6
  102.5 1.9 collective-permute-done.6
  104.4 1.8 collective-permute-done.7
  106.2 0.0 collective-permute-done.8
  106.2 0.0 collective-permute-done.9
  106.2 0.2 fusion.24
  106.5 0.7 multiply_reduce_fusion.4
  107.2 42.0 %all-reduce.2 = (f32[]{:T(128)}, f32[]{:T(128)}) all-reduce(f32[]{:T(128)} %get-tuple-element.54, f32[]{:T(128)} %get-tuple-element.53), channel_id=1, replica_groups=mesh['lat'=4,'lon'=8] {'lat','lon'}, use_global_device_ids=true, to_apply=%region_5.7 | all-reduce | flops 2 | bytes 16 | tf_op jit(solution)/shard_map/psum | solution.py:35
  153.8 0.1 convert_multiply_fusion.1
  153.9 8.1 %all-gather.3 = f32[1,2048]{1,0:T(1,128)S(1)} all-gather(f32[1,256]{1,0:T(1,128)S(1)} %get-tuple-element.80), channel_id=5, replica_groups=mesh['lat'=4,'lon'=8] {'lon'}, dimensions={1}, use_global_device_ids=true | all-gather | bytes 9216 | tf_op jit(solution)/shard_map/all_gather | solution.py:58
  162.0 2.8 collective-permute-start.13
  164.8 0.1 fusion.53
  164.9 1.7 gather_fusion.3
  166.6 3.9 %collective-permute-start.12 = (f32[1,256]{1,0:T(1,128)S(1)}, f32[1,256]{1,0:T(1,128)S(1)}, u32[]{:S(2)}, u32[]{:S(2)}) collective-permute-start(f32[1,256]{1,0:T(1,128)S(1)} %get-tuple-element.79), channel_id=1, source_target_pairs={{8,0},{16,8},{24,16},{9,1},{17,9},{25,17},{10,2},{18,10},{26,18},{... | collective-permute-start | bytes 3080 | tf_op jit(solution)/shard_map/ppermute | solution.py:19
  170.6 1.7 collective-permute-start.10
  172.3 0.0 collective-permute-start.11
  172.3 1.9 collective-permute-done.10
  174.2 1.8 collective-permute-done.11
  176.0 0.0 collective-permute-done.12
  176.0 0.0 collective-permute-done.13
  176.0 0.2 fusion.13
  176.2 0.7 multiply_reduce_fusion.2
  177.0 40.9 %all-reduce.1 = (f32[]{:T(128)}, f32[]{:T(128)}) all-reduce(f32[]{:T(128)} %get-tuple-element.52, f32[]{:T(128)} %get-tuple-element.51), channel_id=1, replica_groups=mesh['lat'=4,'lon'=8] {'lat','lon'}, use_global_device_ids=true, to_apply=%region_9.11 | all-reduce | flops 2 | bytes 16 | tf_op jit(solution)/shard_map/psum | solution.py:35
  221.8 0.1 convert_multiply_fusion
  221.9 8.2 %all-gather.4 = f32[1,2048]{1,0:T(1,128)S(1)} all-gather(f32[1,256]{1,0:T(1,128)S(1)} %get-tuple-element.76), channel_id=6, replica_groups=mesh['lat'=4,'lon'=8] {'lon'}, dimensions={1}, use_global_device_ids=true | all-gather | bytes 9216 | tf_op jit(solution)/shard_map/all_gather | solution.py:58
  230.1 3.8 %collective-permute-start.17 = (f32[1,256]{1,0:T(1,128)S(1)}, f32[1,256]{1,0:T(1,128)S(1)}, u32[]{:S(2)}, u32[]{:S(2)}) collective-permute-start(f32[1,256]{1,0:T(1,128)S(1)} %get-tuple-element.76), channel_id=1, source_target_pairs={{0,8},{8,16},{16,24},{1,9},{9,17},{17,25},{2,10},{10,18},{18,26},{... | collective-permute-start | bytes 3080 | tf_op jit(solution)/shard_map/ppermute | solution.py:17
  233.9 0.1 fusion.51
  234.0 1.7 gather_fusion.4
  235.7 2.9 collective-permute-start.16
  238.6 1.7 collective-permute-start.14
  240.3 1.9 collective-permute-done.14
  242.2 1.8 collective-permute-done.15
  244.0 0.0 collective-permute-done.17
  244.0 0.2 fusion.2
  244.3 0.7 multiply_reduce_fusion
  244.9 42.0 %all-reduce = (f32[]{:T(128)}, f32[]{:T(128)}) all-reduce(f32[]{:T(128)} %get-tuple-element.56, f32[]{:T(128)} %get-tuple-element.55), channel_id=1, replica_groups=mesh['lat'=4,'lon'=8] {'lat','lon'}, use_global_device_ids=true, to_apply=%region_13.15 | all-reduce | flops 2 | bytes 16 | tf_op jit(solution)/shard_map/psum | solution.py:35
  291.0 0.9 multiply_subtract_fusion
  (38 shorter events, 0.4 us)
Async XLA Ops:
  0.6 1.0 copy-start.4
  1.6 35.0 %collective-permute-start.1 = (f32[128,1]{1,0:T(8,128)S(1)}, f32[128,1]{1,0:T(8,128)S(1)}, u32[]{:S(2)}, u32[]{:S(2)}) collective-permute-start(f32[128,1]{1,0:T(8,128)S(1)} %slice.203), channel_id=1, source_target_pairs={{0,1},{1,2},{2,3},{3,4},{4,5},{5,6},{6,7},{7,0},{8,9},{9,10},{10,1... | collective-permute-start | bytes 1544 | tf_op jit(solution)/shard_map/ppermute | solution.py:17
  1.7 3.5 %copy-start = (s32[128,256]{1,0:T(8,128)S(1)}, s32[128,256]{1,0:T(8,128)}, u32[]{:S(2)}) copy-start(s32[128,256]{1,0:T(8,128)} %param.20) | copy-start | bytes 393220
  1.7 3.5 %copy-start.1 = (f32[128,256]{1,0:T(8,128)S(1)}, f32[128,256]{1,0:T(8,128)}, u32[]{:S(2)}) copy-start(f32[128,256]{1,0:T(8,128)} %param.16) | copy-start | bytes 393220
  1.8 38.5 %collective-permute-start.4 = (f32[1,256]{1,0:T(1,128)S(1)}, f32[1,256]{1,0:T(1,128)S(1)}, u32[]{:S(2)}, u32[]{:S(2)}) collective-permute-start(f32[1,256]{1,0:T(1,128)S(1)} %slice.255), channel_id=1, source_target_pairs={{0,8},{8,16},{16,24},{1,9},{9,17},{17,25},{2,10},{10,18},{18,26},{... | collective-permute-start | bytes 3080 | tf_op jit(solution)/shard_map/ppermute | solution.py:17
  5.3 35.0 %collective-permute-start.3 = (f32[1,256]{1,0:T(1,128)S(1)}, f32[1,256]{1,0:T(1,128)S(1)}, u32[]{:S(2)}, u32[]{:S(2)}) collective-permute-start(f32[1,256]{1,0:T(1,128)S(1)} %get-tuple-element.87), channel_id=1, source_target_pairs={{8,0},{16,8},{24,16},{9,1},{17,9},{25,17},{10,2},{18,10},{26,18},{... | collective-permute-start | bytes 3080 | tf_op jit(solution)/shard_map/ppermute | solution.py:19
  8.6 31.7 %collective-permute-start.5 = (f32[1,256]{1,0:T(1,128)S(1)}, f32[1,256]{1,0:T(1,128)S(1)}, u32[]{:S(2)}, u32[]{:S(2)}) collective-permute-start(f32[1,256]{1,0:T(1,128)S(1)} %get-tuple-element.88), channel_id=1, source_target_pairs={{0,8},{8,16},{16,24},{1,9},{9,17},{17,25},{2,10},{10,18},{18,26},{... | collective-permute-start | bytes 3080 | tf_op jit(solution)/shard_map/ppermute | solution.py:17
  11.2 25.8 %collective-permute-start = (f32[128,1]{1,0:T(8,128)S(1)}, f32[128,1]{1,0:T(8,128)S(1)}, u32[]{:S(2)}, u32[]{:S(2)}) collective-permute-start(f32[128,1]{1,0:T(8,128)S(1)} %get-tuple-element.85), channel_id=1, source_target_pairs={{1,0},{2,1},{3,2},{4,3},{5,4},{6,5},{7,6},{0,7},{9,8},{10,9},{11,1... | collective-permute-start | bytes 1544 | tf_op jit(solution)/shard_map/ppermute | solution.py:19
  12.1 10.8 %copy-start.5 = (s32[256]{0:T(256)S(1)}, s32[256]{0:T(256)}, u32[]{:S(2)}) copy-start(s32[256]{0:T(256)} %param.21) | copy-start | bytes 3076
  34.8 5.5 %copy-start.3 = (f32[128,256]{1,0:T(8,128)S(1)}, f32[128,256]{1,0:T(8,128)}, u32[]{:S(2)}) copy-start(f32[128,256]{1,0:T(8,128)} %param.18) | copy-start | bytes 393220
  36.6 3.7 %collective-permute-start.2 = (f32[128,1]{1,0:T(8,128)S(1)}, f32[128,1]{1,0:T(8,128)S(1)}, u32[]{:S(2)}, u32[]{:S(2)}) collective-permute-start(f32[128,1]{1,0:T(8,128)S(1)} %get-tuple-element.86), channel_id=1, source_target_pairs={{0,1},{1,2},{2,3},{3,4},{4,5},{5,6},{6,7},{7,0},{8,9},{9,10},{10,1... | collective-permute-start | bytes 1544 | tf_op jit(solution)/shard_map/ppermute | solution.py:17
  37.0 3.6 %copy-start.2 = (f32[128,256]{1,0:T(8,128)S(1)}, f32[128,256]{1,0:T(8,128)}, u32[]{:S(2)}) copy-start(f32[128,256]{1,0:T(8,128)} %param.17) | copy-start | bytes 393220
  92.4 13.8 %collective-permute-start.9 = (f32[1,256]{1,0:T(1,128)S(1)}, f32[1,256]{1,0:T(1,128)S(1)}, u32[]{:S(2)}, u32[]{:S(2)}) collective-permute-start(f32[1,256]{1,0:T(1,128)S(1)} %get-tuple-element.84), channel_id=1, source_target_pairs={{0,8},{8,16},{16,24},{1,9},{9,17},{17,25},{2,10},{10,18},{18,26},{... | collective-permute-start | bytes 3080 | tf_op jit(solution)/shard_map/ppermute | solution.py:17
  98.1 8.1 %collective-permute-start.8 = (f32[1,256]{1,0:T(1,128)S(1)}, f32[1,256]{1,0:T(1,128)S(1)}, u32[]{:S(2)}, u32[]{:S(2)}) collective-permute-start(f32[1,256]{1,0:T(1,128)S(1)} %get-tuple-element.83), channel_id=1, source_target_pairs={{8,0},{16,8},{24,16},{9,1},{17,9},{25,17},{10,2},{18,10},{26,18},{... | collective-permute-start | bytes 3080 | tf_op jit(solution)/shard_map/ppermute | solution.py:19
  101.0 3.4 %collective-permute-start.6 = (f32[128,1]{1,0:T(8,128)S(1)}, f32[128,1]{1,0:T(8,128)S(1)}, u32[]{:S(2)}, u32[]{:S(2)}) collective-permute-start(f32[128,1]{1,0:T(8,128)S(1)} %get-tuple-element.81), channel_id=1, source_target_pairs={{1,0},{2,1},{3,2},{4,3},{5,4},{6,5},{7,6},{0,7},{9,8},{10,9},{11,1... | collective-permute-start | bytes 1544 | tf_op jit(solution)/shard_map/ppermute | solution.py:19
  102.5 3.7 %collective-permute-start.7 = (f32[128,1]{1,0:T(8,128)S(1)}, f32[128,1]{1,0:T(8,128)S(1)}, u32[]{:S(2)}, u32[]{:S(2)}) collective-permute-start(f32[128,1]{1,0:T(8,128)S(1)} %get-tuple-element.82), channel_id=1, source_target_pairs={{0,1},{1,2},{2,3},{3,4},{4,5},{5,6},{6,7},{7,0},{8,9},{9,10},{10,1... | collective-permute-start | bytes 1544 | tf_op jit(solution)/shard_map/ppermute | solution.py:17
  162.0 14.0 %collective-permute-start.13 = (f32[1,256]{1,0:T(1,128)S(1)}, f32[1,256]{1,0:T(1,128)S(1)}, u32[]{:S(2)}, u32[]{:S(2)}) collective-permute-start(f32[1,256]{1,0:T(1,128)S(1)} %get-tuple-element.80), channel_id=1, source_target_pairs={{0,8},{8,16},{16,24},{1,9},{9,17},{17,25},{2,10},{10,18},{18,26},{... | collective-permute-start | bytes 3080 | tf_op jit(solution)/shard_map/ppermute | solution.py:17
  166.6 9.4 %collective-permute-start.12 = (f32[1,256]{1,0:T(1,128)S(1)}, f32[1,256]{1,0:T(1,128)S(1)}, u32[]{:S(2)}, u32[]{:S(2)}) collective-permute-start(f32[1,256]{1,0:T(1,128)S(1)} %get-tuple-element.79), channel_id=1, source_target_pairs={{8,0},{16,8},{24,16},{9,1},{17,9},{25,17},{10,2},{18,10},{26,18},{... | collective-permute-start | bytes 3080 | tf_op jit(solution)/shard_map/ppermute | solution.py:19
  170.6 3.6 %collective-permute-start.10 = (f32[128,1]{1,0:T(8,128)S(1)}, f32[128,1]{1,0:T(8,128)S(1)}, u32[]{:S(2)}, u32[]{:S(2)}) collective-permute-start(f32[128,1]{1,0:T(8,128)S(1)} %get-tuple-element.77), channel_id=1, source_target_pairs={{1,0},{2,1},{3,2},{4,3},{5,4},{6,5},{7,6},{0,7},{9,8},{10,9},{11,1... | collective-permute-start | bytes 1544 | tf_op jit(solution)/shard_map/ppermute | solution.py:19
  172.3 3.7 %collective-permute-start.11 = (f32[128,1]{1,0:T(8,128)S(1)}, f32[128,1]{1,0:T(8,128)S(1)}, u32[]{:S(2)}, u32[]{:S(2)}) collective-permute-start(f32[128,1]{1,0:T(8,128)S(1)} %get-tuple-element.78), channel_id=1, source_target_pairs={{0,1},{1,2},{2,3},{3,4},{4,5},{5,6},{6,7},{7,0},{8,9},{9,10},{10,1... | collective-permute-start | bytes 1544 | tf_op jit(solution)/shard_map/ppermute | solution.py:17
  230.1 13.9 %collective-permute-start.17 = (f32[1,256]{1,0:T(1,128)S(1)}, f32[1,256]{1,0:T(1,128)S(1)}, u32[]{:S(2)}, u32[]{:S(2)}) collective-permute-start(f32[1,256]{1,0:T(1,128)S(1)} %get-tuple-element.76), channel_id=1, source_target_pairs={{0,8},{8,16},{16,24},{1,9},{9,17},{17,25},{2,10},{10,18},{18,26},{... | collective-permute-start | bytes 3080 | tf_op jit(solution)/shard_map/ppermute | solution.py:17
  235.7 8.3 %collective-permute-start.16 = (f32[1,256]{1,0:T(1,128)S(1)}, f32[1,256]{1,0:T(1,128)S(1)}, u32[]{:S(2)}, u32[]{:S(2)}) collective-permute-start(f32[1,256]{1,0:T(1,128)S(1)} %get-tuple-element.75), channel_id=1, source_target_pairs={{8,0},{16,8},{24,16},{9,1},{17,9},{25,17},{10,2},{18,10},{26,18},{... | collective-permute-start | bytes 3080 | tf_op jit(solution)/shard_map/ppermute | solution.py:19
  238.6 3.6 %collective-permute-start.14 = (f32[128,1]{1,0:T(8,128)S(1)}, f32[128,1]{1,0:T(8,128)S(1)}, u32[]{:S(2)}, u32[]{:S(2)}) collective-permute-start(f32[128,1]{1,0:T(8,128)S(1)} %get-tuple-element.73), channel_id=1, source_target_pairs={{1,0},{2,1},{3,2},{4,3},{5,4},{6,5},{7,6},{0,7},{9,8},{10,9},{11,1... | collective-permute-start | bytes 1544 | tf_op jit(solution)/shard_map/ppermute | solution.py:19
  240.3 3.7 %collective-permute-start.15 = (f32[128,1]{1,0:T(8,128)S(1)}, f32[128,1]{1,0:T(8,128)S(1)}, u32[]{:S(2)}, u32[]{:S(2)}) collective-permute-start(f32[128,1]{1,0:T(8,128)S(1)} %get-tuple-element.74), channel_id=1, source_target_pairs={{0,1},{1,2},{2,3},{3,4},{4,5},{5,6},{6,7},{7,0},{8,9},{9,10},{10,1... | collective-permute-start | bytes 1544 | tf_op jit(solution)/shard_map/ppermute | solution.py:17
where the time goes:
time: 293 us; the launch traced here: 292 us
  blocking collectives  212 us (72%)
  starting transfers between devices  35.7 us (12%)
  between operations  14.9 us (5%)
  waiting for transfers between devices  14.4 us (5%)
  local copies, waits for them, and re-layouts  10.1 us (3%)
  other arithmetic  4.81 us (2%)
    psum x4, blocking collectives, paired(): lax.psum((jnp.sum(residual * residual), jnp.sum(residual * image)), ('lat...  166 us
    all_gather x5, blocking collectives, mirror_row(): whole_row = lax.all_gather(top_values, 'lon', axis=0, tiled=True)  45.7 us
    ppermute x8, starting transfers between devices, with_halo(): lax.ppermute(head, axis, [((i + 1) % count, i) for i in range(ends)])  18.9 us
    ppermute x10, starting transfers between devices, with_halo(): lax.ppermute(tail, axis, [(i, (i + 1) % count) for i in range(ends)])  16.8 us
    ppermute x10, waiting for transfers between devices, with_halo(): lax.ppermute(tail, axis, [(i, (i + 1) % count) for i in range(ends)])  8.69 us
    gather x5, local copies, waits for them, and re-layouts, mirror_row(): return jnp.take(whole_row, fold_partner, axis=0)  8.62 us
  transfers between devices with their start and end apart: 18, of which 7 were waited for; matrix products, arithmetic and copies ran while one was open for 3% of the time, Pallas kernels for 0%

commit v1 on v0

--- a/solution.py
+++ b/solution.py
@@ -55,7 +55,10 @@
         )
 
     def mirror_row(top_values):
-        whole_row = lax.all_gather(top_values, "lon", axis=0, tiled=True)
+        size = lax.axis_size("lon")
+        blocks = jnp.stack([top_values for _ in range(size)])
+        blocks = lax.all_to_all(blocks, "lon", split_axis=0, concat_axis=0)
+        whole_row = jnp.concatenate(blocks, axis=0)
         return jnp.take(whole_row, fold_partner, axis=0)
 
     top_coef = north_coef[row_count - 1]

time: 293 us -> 270 us (0.922)
  blocking collectives: 212 us -> 163 us
  starting transfers between devices: 35.7 us -> 56.6 us
  local copies, waits for them, and re-layouts: 10.1 us -> 13.8 us
    all_gather x5 -> x0, blocking collectives: 45.7 us -> none  [mirror_row(): whole_row = lax.all_gather(top_values, 'lon', axis=0, tiled=True)]
    all_to_all x0 -> x5, starting transfers between devices: none -> 26.7 us  [mirror_row(): blocks = lax.all_to_all(blocks, 'lon', split_axis=0, concat_axis=0)]
    all_to_all x0 -> x5, waiting for transfers between devices: none -> 14 us  [mirror_row(): blocks = lax.all_to_all(blocks, 'lon', split_axis=0, concat_axis=0)]
    ppermute x10, waiting for transfers between devices: 8.69 us -> 0.03 us  [with_halo(): lax.ppermute(tail, axis, [(i, (i + 1) % count) for i in range(ends)])]
    ppermute x8, waiting for transfers between devices: 5.69 us -> 0.02 us  [with_halo(): lax.ppermute(head, axis, [((i + 1) % count, i) for i in range(ends)])]
    ppermute x8, starting transfers between devices: 18.9 us -> 13.7 us  [with_halo(): lax.ppermute(head, axis, [((i + 1) % count, i) for i in range(ends)])]
    psum x4, blocking collectives: 166 us -> 163 us  [paired(): lax.psum((jnp.sum(residual * residual), jnp.sum(residual * image)), ('lat...]
    another operation x0 -> x5, local copies, waits for them, and re-layouts: none -> 3.02 us  [mirror_row(): blocks = jnp.stack([top_values for _ in range(size)])]
  transfers between devices with their start and end apart: 18 -> 23, of which waited for: 7 -> 4; matrix products, arithmetic and copies ran while one was open for 3% -> 2% of each run, Pallas kernels for 0% -> 0%
where the time goes in v1:
time: 270 us; the launch traced here: 267 us
  blocking collectives  163 us (60%)
  starting transfers between devices  56.6 us (21%)
  between operations  15.1 us (6%)
  waiting for transfers between devices  14.1 us (5%)
  local copies, waits for them, and re-layouts  13.8 us (5%)
  other arithmetic  4.81 us (2%)
    psum x4, blocking collectives, paired(): lax.psum((jnp.sum(residual * residual), jnp.sum(residual * image)), ('lat...  163 us
    all_to_all x5, starting transfers between devices, mirror_row(): blocks = lax.all_to_all(blocks, 'lon', split_axis=0, concat_axis=0)  26.7 us
    ppermute x10, starting transfers between devices, with_halo(): lax.ppermute(tail, axis, [(i, (i + 1) % count) for i in range(ends)])  16.2 us
    all_to_all x5, waiting for transfers between devices, mirror_row(): blocks = lax.all_to_all(blocks, 'lon', split_axis=0, concat_axis=0)  14 us
    ppermute x8, starting transfers between devices, with_halo(): lax.ppermute(head, axis, [((i + 1) % count, i) for i in range(ends)])  13.7 us
    gather x5, local copies, waits for them, and re-layouts, mirror_row(): return jnp.take(whole_row, fold_partner, axis=0)  8.6 us
  transfers between devices with their start and end apart: 23, of which 4 were waited for; matrix products, arithmetic and copies ran while one was open for 2% of the time, Pallas kernels for 0%

profile of v1, /device:TPU:12, one launch (start us, length us, event | category | flops | bytes accessed | tf_op | source)
XLA Modules:
  0.0 267.5 jit_solution(13068125819222462051)
XLA Ops:
  0.6 0.8 slice.214
  1.4 0.6 stack.15
  2.0 5.3 %all-to-all-start = ((f32[8,1,256]{2,1,0:T(1,128)}), f32[8,1,256]{2,1,0:T(1,128)S(1)}, u32[]{:S(2)}, u32[]{:S(2)}) async-start(f32[8,1,256]{2,1,0:T(1,128)} %stack.15), calls=%async_computation | async-start | bytes 16384 | tf_op jit(solution)/shard_map/all_to_all | solution.py:60
  7.3 0.9 slice.203
  8.2 0.2 collective-permute-start.1
  8.4 0.0 copy-start.1
  8.4 0.1 broadcast_select_fusion
  8.5 3.4 %collective-permute-start.4 = (f32[1,256]{1,0:T(1,128)S(1)}, f32[1,256]{1,0:T(1,128)S(1)}, u32[]{:S(2)}, u32[]{:S(2)}) collective-permute-start(f32[1,256]{1,0:T(1,128)S(1)} %slice.255), channel_id=1, source_target_pairs={{0,8},{8,16},{16,24},{1,9},{9,17},{17,25},{2,10},{10,18},{18,26},{... | collective-permute-start | bytes 3080 | tf_op jit(solution)/shard_map/ppermute | solution.py:17
  12.0 3.3 %collective-permute-start.3 = (f32[1,256]{1,0:T(1,128)S(1)}, f32[1,256]{1,0:T(1,128)S(1)}, u32[]{:S(2)}, u32[]{:S(2)}) collective-permute-start(f32[1,256]{1,0:T(1,128)S(1)} %get-tuple-element.87), channel_id=1, source_target_pairs={{8,0},{16,8},{24,16},{9,1},{17,9},{25,17},{10,2},{18,10},{26,18},{... | collective-permute-start | bytes 3080 | tf_op jit(solution)/shard_map/ppermute | solution.py:19
  15.3 0.0 copy-start.3
  15.4 2.6 collective-permute-start.5
  18.0 0.1 fusion.57
  18.1 0.8 collective-permute-start
  18.9 0.5 collective-permute-start.2
  19.4 0.6 stack.16
  20.0 6.2 %all-to-all-start.1 = ((f32[8,1,256]{2,1,0:T(1,128)}), f32[8,1,256]{2,1,0:T(1,128)S(1)}, u32[]{:S(2)}, u32[]{:S(2)}) async-start(f32[8,1,256]{2,1,0:T(1,128)} %stack.16), calls=%async_computation.1 | async-start | bytes 16384 | tf_op jit(solution)/shard_map/all_to_all | solution.py:60
  26.3 0.0 collective-permute-done.4
  26.3 0.2 fusion.35
  26.5 1.7 gather_fusion
  28.2 2.2 all-to-all-done.1
  30.4 1.7 gather_fusion.1
  32.3 0.7 multiply_reduce_fusion.6
  32.9 40.7 %all-reduce.3 = (f32[]{:T(128)}, f32[]{:T(128)}) all-reduce(f32[]{:T(128)} %get-tuple-element.58, f32[]{:T(128)} %get-tuple-element.57), channel_id=1, replica_groups=mesh['lat'=4,'lon'=8] {'lat','lon'}, use_global_device_ids=true, to_apply=%region_1.2 | all-reduce | flops 2 | bytes 16 | tf_op jit(solution)/shard_map/psum | solution.py:35
  74.9 3.2 %collective-permute-start.8 = (f32[1,256]{1,0:T(1,128)S(1)}, f32[1,256]{1,0:T(1,128)S(1)}, u32[]{:S(2)}, u32[]{:S(2)}) collective-permute-start(f32[1,256]{1,0:T(1,128)S(1)} %get-tuple-element.83), channel_id=1, source_target_pairs={{8,0},{16,8},{24,16},{9,1},{17,9},{25,17},{10,2},{18,10},{26,18},{... | collective-permute-start | bytes 3080 | tf_op jit(solution)/shard_map/ppermute | solution.py:19
  78.1 2.7 collective-permute-start.9
  80.8 0.1 fusion.55
  80.9 0.0 collective-permute-start.6
  80.9 0.5 collective-permute-start.7
  81.4 0.6 stack.17
  82.0 5.0 %all-to-all-start.2 = ((f32[8,1,256]{2,1,0:T(1,128)}), f32[8,1,256]{2,1,0:T(1,128)S(1)}, u32[]{:S(2)}, u32[]{:S(2)}) async-start(f32[8,1,256]{2,1,0:T(1,128)} %stack.17), calls=%async_computation.2 | async-start | bytes 16384 | tf_op jit(solution)/shard_map/all_to_all | solution.py:60
  87.0 0.0 collective-permute-done.6
  87.0 0.0 collective-permute-done.8
  87.1 0.2 fusion.24
  87.3 3.9 %all-to-all-done.2 = f32[8,1,256]{2,1,0:T(1,128)S(1)} async-done(((f32[8,1,256]{2,1,0:T(1,128)}), f32[8,1,256]{2,1,0:T(1,128)S(1)}, u32[]{:S(2)}, u32[]{:S(2)}) %all-to-all-start.2) | async-done | bytes 8224 | tf_op jit(solution)/shard_map/all_to_all | solution.py:60
  91.2 1.7 gather_fusion.2
  93.0 0.8 multiply_reduce_fusion.4
  93.8 40.8 %all-reduce.2 = (f32[]{:T(128)}, f32[]{:T(128)}) all-reduce(f32[]{:T(128)} %get-tuple-element.54, f32[]{:T(128)} %get-tuple-element.53), channel_id=1, replica_groups=mesh['lat'=4,'lon'=8] {'lat','lon'}, use_global_device_ids=true, to_apply=%region_5.7 | all-reduce | flops 2 | bytes 16 | tf_op jit(solution)/shard_map/psum | solution.py:35
  139.2 0.1 convert_multiply_fusion.1
  139.3 3.1 %collective-permute-start.12 = (f32[1,256]{1,0:T(1,128)S(1)}, f32[1,256]{1,0:T(1,128)S(1)}, u32[]{:S(2)}, u32[]{:S(2)}) collective-permute-start(f32[1,256]{1,0:T(1,128)S(1)} %get-tuple-element.79), channel_id=1, source_target_pairs={{8,0},{16,8},{24,16},{9,1},{17,9},{25,17},{10,2},{18,10},{26,18},{... | collective-permute-start | bytes 3080 | tf_op jit(solution)/shard_map/ppermute | solution.py:19
  142.4 2.7 %collective-permute-start.13 = (f32[1,256]{1,0:T(1,128)S(1)}, f32[1,256]{1,0:T(1,128)S(1)}, u32[]{:S(2)}, u32[]{:S(2)}) collective-permute-start(f32[1,256]{1,0:T(1,128)S(1)} %get-tuple-element.80), channel_id=1, source_target_pairs={{0,8},{8,16},{16,24},{1,9},{9,17},{17,25},{2,10},{10,18},{18,26},{... | collective-permute-start | bytes 3080 | tf_op jit(solution)/shard_map/ppermute | solution.py:17
  145.2 0.1 fusion.53
  145.2 0.0 collective-permute-start.10
  145.3 0.5 collective-permute-start.11
  145.8 0.6 stack.18
  146.4 5.0 %all-to-all-start.3 = ((f32[8,1,256]{2,1,0:T(1,128)}), f32[8,1,256]{2,1,0:T(1,128)S(1)}, u32[]{:S(2)}, u32[]{:S(2)}) async-start(f32[8,1,256]{2,1,0:T(1,128)} %stack.18), calls=%async_computation.3 | async-start | bytes 16384 | tf_op jit(solution)/shard_map/all_to_all | solution.py:60
  151.4 0.2 fusion.13
  151.6 3.9 %all-to-all-done.3 = f32[8,1,256]{2,1,0:T(1,128)S(1)} async-done(((f32[8,1,256]{2,1,0:T(1,128)}), f32[8,1,256]{2,1,0:T(1,128)S(1)}, u32[]{:S(2)}, u32[]{:S(2)}) %all-to-all-start.3) | async-done | bytes 8224 | tf_op jit(solution)/shard_map/all_to_all | solution.py:60
  155.6 1.7 gather_fusion.3
  157.4 0.7 multiply_reduce_fusion.2
  158.1 40.7 %all-reduce.1 = (f32[]{:T(128)}, f32[]{:T(128)}) all-reduce(f32[]{:T(128)} %get-tuple-element.52, f32[]{:T(128)} %get-tuple-element.51), channel_id=1, replica_groups=mesh['lat'=4,'lon'=8] {'lat','lon'}, use_global_device_ids=true, to_apply=%region_9.11 | all-reduce | flops 2 | bytes 16 | tf_op jit(solution)/shard_map/psum | solution.py:35
  202.9 0.1 convert_multiply_fusion
  203.0 3.2 %collective-permute-start.16 = (f32[1,256]{1,0:T(1,128)S(1)}, f32[1,256]{1,0:T(1,128)S(1)}, u32[]{:S(2)}, u32[]{:S(2)}) collective-permute-start(f32[1,256]{1,0:T(1,128)S(1)} %get-tuple-element.75), channel_id=1, source_target_pairs={{8,0},{16,8},{24,16},{9,1},{17,9},{25,17},{10,2},{18,10},{26,18},{... | collective-permute-start | bytes 3080 | tf_op jit(solution)/shard_map/ppermute | solution.py:19
  206.2 2.7 collective-permute-start.17
  208.9 0.1 fusion.51
  208.9 0.0 collective-permute-start.14
  209.0 0.5 collective-permute-start.15
  209.5 0.6 stack.19
  210.1 5.0 %all-to-all-start.4 = ((f32[8,1,256]{2,1,0:T(1,128)}), f32[8,1,256]{2,1,0:T(1,128)S(1)}, u32[]{:S(2)}, u32[]{:S(2)}) async-start(f32[8,1,256]{2,1,0:T(1,128)} %stack.19), calls=%async_computation.4 | async-start | bytes 16384 | tf_op jit(solution)/shard_map/all_to_all | solution.py:60
  215.1 0.2 fusion.2
  215.3 3.9 %all-to-all-done.4 = f32[8,1,256]{2,1,0:T(1,128)S(1)} async-done(((f32[8,1,256]{2,1,0:T(1,128)}), f32[8,1,256]{2,1,0:T(1,128)S(1)}, u32[]{:S(2)}, u32[]{:S(2)}) %all-to-all-start.4) | async-done | bytes 8224 | tf_op jit(solution)/shard_map/all_to_all | solution.py:60
  219.3 1.7 gather_fusion.4
  221.1 0.6 multiply_reduce_fusion
  221.7 40.8 %all-reduce = (f32[]{:T(128)}, f32[]{:T(128)}) all-reduce(f32[]{:T(128)} %get-tuple-element.56, f32[]{:T(128)} %get-tuple-element.55), channel_id=1, replica_groups=mesh['lat'=4,'lon'=8] {'lat','lon'}, use_global_device_ids=true, to_apply=%region_13.15 | all-reduce | flops 2 | bytes 16 | tf_op jit(solution)/shard_map/psum | solution.py:35
  266.6 0.9 multiply_subtract_fusion
  (48 shorter events, 0.4 us)
Async XLA Ops:
  0.6 7.8 %copy-start.4 = (f32[128,256]{1,0:T(8,128)S(1)}, f32[128,256]{1,0:T(8,128)}, u32[]{:S(2)}) copy-start(f32[128,256]{1,0:T(8,128)} %param.19) | copy-start | bytes 393220
  2.0 17.4 %all-to-all-start = ((f32[8,1,256]{2,1,0:T(1,128)}), f32[8,1,256]{2,1,0:T(1,128)S(1)}, u32[]{:S(2)}, u32[]{:S(2)}) async-start(f32[8,1,256]{2,1,0:T(1,128)} %stack.15), calls=%async_computation | async-start | bytes 16384 | tf_op jit(solution)/shard_map/all_to_all | solution.py:60
  8.2 10.7 %collective-permute-start.1 = (f32[128,1]{1,0:T(8,128)S(1)}, f32[128,1]{1,0:T(8,128)S(1)}, u32[]{:S(2)}, u32[]{:S(2)}) collective-permute-start(f32[128,1]{1,0:T(8,128)S(1)} %slice.203), channel_id=1, source_target_pairs={{0,1},{1,2},{2,3},{3,4},{4,5},{5,6},{6,7},{7,0},{8,9},{9,10},{10,1... | collective-permute-start | bytes 1544 | tf_op jit(solution)/shard_map/ppermute | solution.py:17
  8.4 3.5 %copy-start = (s32[128,256]{1,0:T(8,128)S(1)}, s32[128,256]{1,0:T(8,128)}, u32[]{:S(2)}) copy-start(s32[128,256]{1,0:T(8,128)} %param.20) | copy-start | bytes 393220
  8.4 3.5 %copy-start.1 = (f32[128,256]{1,0:T(8,128)S(1)}, f32[128,256]{1,0:T(8,128)}, u32[]{:S(2)}) copy-start(f32[128,256]{1,0:T(8,128)} %param.16) | copy-start | bytes 393220
  8.5 17.7 %collective-permute-start.4 = (f32[1,256]{1,0:T(1,128)S(1)}, f32[1,256]{1,0:T(1,128)S(1)}, u32[]{:S(2)}, u32[]{:S(2)}) collective-permute-start(f32[1,256]{1,0:T(1,128)S(1)} %slice.255), channel_id=1, source_target_pairs={{0,8},{8,16},{16,24},{1,9},{9,17},{17,25},{2,10},{10,18},{18,26},{... | collective-permute-start | bytes 3080 | tf_op jit(solution)/shard_map/ppermute | solution.py:17
  12.0 14.3 %collective-permute-start.3 = (f32[1,256]{1,0:T(1,128)S(1)}, f32[1,256]{1,0:T(1,128)S(1)}, u32[]{:S(2)}, u32[]{:S(2)}) collective-permute-start(f32[1,256]{1,0:T(1,128)S(1)} %get-tuple-element.87), channel_id=1, source_target_pairs={{8,0},{16,8},{24,16},{9,1},{17,9},{25,17},{10,2},{18,10},{26,18},{... | collective-permute-start | bytes 3080 | tf_op jit(solution)/shard_map/ppermute | solution.py:19
  15.3 11.0 %copy-start.3 = (f32[128,256]{1,0:T(8,128)S(1)}, f32[128,256]{1,0:T(8,128)}, u32[]{:S(2)}) copy-start(f32[128,256]{1,0:T(8,128)} %param.18) | copy-start | bytes 393220
  15.4 10.9 %collective-permute-start.5 = (f32[1,256]{1,0:T(1,128)S(1)}, f32[1,256]{1,0:T(1,128)S(1)}, u32[]{:S(2)}, u32[]{:S(2)}) collective-permute-start(f32[1,256]{1,0:T(1,128)S(1)} %get-tuple-element.88), channel_id=1, source_target_pairs={{0,8},{8,16},{16,24},{1,9},{9,17},{17,25},{2,10},{10,18},{18,26},{... | collective-permute-start | bytes 3080 | tf_op jit(solution)/shard_map/ppermute | solution.py:17
  18.1 0.8 copy-start.5
  18.1 8.2 %collective-permute-start = (f32[128,1]{1,0:T(8,128)S(1)}, f32[128,1]{1,0:T(8,128)S(1)}, u32[]{:S(2)}, u32[]{:S(2)}) collective-permute-start(f32[128,1]{1,0:T(8,128)S(1)} %get-tuple-element.85), channel_id=1, source_target_pairs={{1,0},{2,1},{3,2},{4,3},{5,4},{6,5},{7,6},{0,7},{9,8},{10,9},{11,1... | collective-permute-start | bytes 1544 | tf_op jit(solution)/shard_map/ppermute | solution.py:19
  18.9 7.3 %collective-permute-start.2 = (f32[128,1]{1,0:T(8,128)S(1)}, f32[128,1]{1,0:T(8,128)S(1)}, u32[]{:S(2)}, u32[]{:S(2)}) collective-permute-start(f32[128,1]{1,0:T(8,128)S(1)} %get-tuple-element.86), channel_id=1, source_target_pairs={{0,1},{1,2},{2,3},{3,4},{4,5},{5,6},{6,7},{7,0},{8,9},{9,10},{10,1... | collective-permute-start | bytes 1544 | tf_op jit(solution)/shard_map/ppermute | solution.py:17
  20.0 10.4 %all-to-all-start.1 = ((f32[8,1,256]{2,1,0:T(1,128)}), f32[8,1,256]{2,1,0:T(1,128)S(1)}, u32[]{:S(2)}, u32[]{:S(2)}) async-start(f32[8,1,256]{2,1,0:T(1,128)} %stack.16), calls=%async_computation.1 | async-start | bytes 16384 | tf_op jit(solution)/shard_map/all_to_all | solution.py:60
  30.4 1.8 copy-start.2
  74.9 12.1 %collective-permute-start.8 = (f32[1,256]{1,0:T(1,128)S(1)}, f32[1,256]{1,0:T(1,128)S(1)}, u32[]{:S(2)}, u32[]{:S(2)}) collective-permute-start(f32[1,256]{1,0:T(1,128)S(1)} %get-tuple-element.83), channel_id=1, source_target_pairs={{8,0},{16,8},{24,16},{9,1},{17,9},{25,17},{10,2},{18,10},{26,18},{... | collective-permute-start | bytes 3080 | tf_op jit(solution)/shard_map/ppermute | solution.py:19
  78.1 8.9 %collective-permute-start.9 = (f32[1,256]{1,0:T(1,128)S(1)}, f32[1,256]{1,0:T(1,128)S(1)}, u32[]{:S(2)}, u32[]{:S(2)}) collective-permute-start(f32[1,256]{1,0:T(1,128)S(1)} %get-tuple-element.84), channel_id=1, source_target_pairs={{0,8},{8,16},{16,24},{1,9},{9,17},{17,25},{2,10},{10,18},{18,26},{... | collective-permute-start | bytes 3080 | tf_op jit(solution)/shard_map/ppermute | solution.py:17
  80.9 6.2 %collective-permute-start.6 = (f32[128,1]{1,0:T(8,128)S(1)}, f32[128,1]{1,0:T(8,128)S(1)}, u32[]{:S(2)}, u32[]{:S(2)}) collective-permute-start(f32[128,1]{1,0:T(8,128)S(1)} %get-tuple-element.81), channel_id=1, source_target_pairs={{1,0},{2,1},{3,2},{4,3},{5,4},{6,5},{7,6},{0,7},{9,8},{10,9},{11,1... | collective-permute-start | bytes 1544 | tf_op jit(solution)/shard_map/ppermute | solution.py:19
  80.9 6.1 %collective-permute-start.7 = (f32[128,1]{1,0:T(8,128)S(1)}, f32[128,1]{1,0:T(8,128)S(1)}, u32[]{:S(2)}, u32[]{:S(2)}) collective-permute-start(f32[128,1]{1,0:T(8,128)S(1)} %get-tuple-element.82), channel_id=1, source_target_pairs={{0,1},{1,2},{2,3},{3,4},{4,5},{5,6},{6,7},{7,0},{8,9},{9,10},{10,1... | collective-permute-start | bytes 1544 | tf_op jit(solution)/shard_map/ppermute | solution.py:17
  82.0 9.2 %all-to-all-start.2 = ((f32[8,1,256]{2,1,0:T(1,128)}), f32[8,1,256]{2,1,0:T(1,128)S(1)}, u32[]{:S(2)}, u32[]{:S(2)}) async-start(f32[8,1,256]{2,1,0:T(1,128)} %stack.17), calls=%async_computation.2 | async-start | bytes 16384 | tf_op jit(solution)/shard_map/all_to_all | solution.py:60
  139.3 12.1 %collective-permute-start.12 = (f32[1,256]{1,0:T(1,128)S(1)}, f32[1,256]{1,0:T(1,128)S(1)}, u32[]{:S(2)}, u32[]{:S(2)}) collective-permute-start(f32[1,256]{1,0:T(1,128)S(1)} %get-tuple-element.79), channel_id=1, source_target_pairs={{8,0},{16,8},{24,16},{9,1},{17,9},{25,17},{10,2},{18,10},{26,18},{... | collective-permute-start | bytes 3080 | tf_op jit(solution)/shard_map/ppermute | solution.py:19
  142.4 9.0 %collective-permute-start.13 = (f32[1,256]{1,0:T(1,128)S(1)}, f32[1,256]{1,0:T(1,128)S(1)}, u32[]{:S(2)}, u32[]{:S(2)}) collective-permute-start(f32[1,256]{1,0:T(1,128)S(1)} %get-tuple-element.80), channel_id=1, source_target_pairs={{0,8},{8,16},{16,24},{1,9},{9,17},{17,25},{2,10},{10,18},{18,26},{... | collective-permute-start | bytes 3080 | tf_op jit(solution)/shard_map/ppermute | solution.py:17
  145.2 6.2 %collective-permute-start.10 = (f32[128,1]{1,0:T(8,128)S(1)}, f32[128,1]{1,0:T(8,128)S(1)}, u32[]{:S(2)}, u32[]{:S(2)}) collective-permute-start(f32[128,1]{1,0:T(8,128)S(1)} %get-tuple-element.77), channel_id=1, source_target_pairs={{1,0},{2,1},{3,2},{4,3},{5,4},{6,5},{7,6},{0,7},{9,8},{10,9},{11,1... | collective-permute-start | bytes 1544 | tf_op jit(solution)/shard_map/ppermute | solution.py:19
  145.3 6.1 %collective-permute-start.11 = (f32[128,1]{1,0:T(8,128)S(1)}, f32[128,1]{1,0:T(8,128)S(1)}, u32[]{:S(2)}, u32[]{:S(2)}) collective-permute-start(f32[128,1]{1,0:T(8,128)S(1)} %get-tuple-element.78), channel_id=1, source_target_pairs={{0,1},{1,2},{2,3},{3,4},{4,5},{5,6},{6,7},{7,0},{8,9},{9,10},{10,1... | collective-permute-start | bytes 1544 | tf_op jit(solution)/shard_map/ppermute | solution.py:17
  146.4 9.2 %all-to-all-start.3 = ((f32[8,1,256]{2,1,0:T(1,128)}), f32[8,1,256]{2,1,0:T(1,128)S(1)}, u32[]{:S(2)}, u32[]{:S(2)}) async-start(f32[8,1,256]{2,1,0:T(1,128)} %stack.18), calls=%async_computation.3 | async-start | bytes 16384 | tf_op jit(solution)/shard_map/all_to_all | solution.py:60
  203.0 12.1 %collective-permute-start.16 = (f32[1,256]{1,0:T(1,128)S(1)}, f32[1,256]{1,0:T(1,128)S(1)}, u32[]{:S(2)}, u32[]{:S(2)}) collective-permute-start(f32[1,256]{1,0:T(1,128)S(1)} %get-tuple-element.75), channel_id=1, source_target_pairs={{8,0},{16,8},{24,16},{9,1},{17,9},{25,17},{10,2},{18,10},{26,18},{... | collective-permute-start | bytes 3080 | tf_op jit(solution)/shard_map/ppermute | solution.py:19
  206.2 8.9 %collective-permute-start.17 = (f32[1,256]{1,0:T(1,128)S(1)}, f32[1,256]{1,0:T(1,128)S(1)}, u32[]{:S(2)}, u32[]{:S(2)}) collective-permute-start(f32[1,256]{1,0:T(1,128)S(1)} %get-tuple-element.76), channel_id=1, source_target_pairs={{0,8},{8,16},{16,24},{1,9},{9,17},{17,25},{2,10},{10,18},{18,26},{... | collective-permute-start | bytes 3080 | tf_op jit(solution)/shard_map/ppermute | solution.py:17
  208.9 6.2 %collective-permute-start.14 = (f32[128,1]{1,0:T(8,128)S(1)}, f32[128,1]{1,0:T(8,128)S(1)}, u32[]{:S(2)}, u32[]{:S(2)}) collective-permute-start(f32[128,1]{1,0:T(8,128)S(1)} %get-tuple-element.73), channel_id=1, source_target_pairs={{1,0},{2,1},{3,2},{4,3},{5,4},{6,5},{7,6},{0,7},{9,8},{10,9},{11,1... | collective-permute-start | bytes 1544 | tf_op jit(solution)/shard_map/ppermute | solution.py:19
  209.0 6.1 %collective-permute-start.15 = (f32[128,1]{1,0:T(8,128)S(1)}, f32[128,1]{1,0:T(8,128)S(1)}, u32[]{:S(2)}, u32[]{:S(2)}) collective-permute-start(f32[128,1]{1,0:T(8,128)S(1)} %get-tuple-element.74), channel_id=1, source_target_pairs={{0,1},{1,2},{2,3},{3,4},{4,5},{5,6},{6,7},{7,0},{8,9},{9,10},{10,1... | collective-permute-start | bytes 1544 | tf_op jit(solution)/shard_map/ppermute | solution.py:17
  210.1 9.2 %all-to-all-start.4 = ((f32[8,1,256]{2,1,0:T(1,128)}), f32[8,1,256]{2,1,0:T(1,128)S(1)}, u32[]{:S(2)}, u32[]{:S(2)}) async-start(f32[8,1,256]{2,1,0:T(1,128)} %stack.19), calls=%async_computation.4 | async-start | bytes 16384 | tf_op jit(solution)/shard_map/all_to_all | solution.py:60
